TPU v7x, 512 devices: a whole 4x8x8 slice. The times are simulated.
512 devices in a mesh: px: 16 (over z, core), py: 32 (over x, y).
Axes of the slice: x: 4, y: 8, z: 8, core: 2. Of those that a mesh axis runs over, the one named last changes fastest.
Arguments:
- field_in: bfloat16 [32, 32, 512, 512], P(None, 'py', 'px'), may hold values from -6 to 6
- cotangent: bfloat16 [32, 32, 512, 512], P(None, 'py', 'px'), may hold values from -6 to 6
- spectrum_saved: float32 [32, 32, 32, 32, 2], P(None, None, 'px', 'py'), may hold values from -6 to 6
- weight_store: float32 [2048, 2, 32, 32], P(('px', 'py')), may hold values from -4.2 to 4.2
- block_slot: int32 [32, 32], P('py', 'px'), may hold values from 0 to 127, as said below
- kx_modes: int32 [32], replicated, may hold values from 0 to 511, as said below
- ky_modes: int32 [32], replicated, may hold values from 0 to 511, as said below
- pointwise: bfloat16 [32, 32], replicated, may hold values from -0.25 to 0.25
- bias_vector: float32 [32], replicated, may hold values from -3 to 3
Outputs:
- field_grad: float32 [32, 32, 512, 512], P(None, 'py', 'px')
- store_grad: float32 [2048, 2, 32, 32], P(('px', 'py'))
Inputs may be any that keep to these rules, and one draw needn't show every extreme that they name: `kx_modes`: 32 distinct wave numbers k, each with k < 32 or k > 480. `ky_modes`: 32 distinct wave numbers k, each with k < 32 or k > 480. `block_slot`: within each px index's 2 second-dimension modes, the values over all 32 x 2 mode pairs are distinct; v // 4 is the py index of the device that stores the block and v % 4 its slot there; in each such group one py index stores 4 blocks, and the other slots hold unused blocks.
All inputs are finite; a program needn't handle non-finite values.
Results may differ from a plain program's by a relative error of at most 0.0003.
Values sent between devices are 32-bit elements; how exact they have to be, the bound alone decides.
A program may use at most 64 MiB of HBM per device.

v0:
```python
import math
import jax
import jax.numpy as jnp
from jax import lax
from jax.sharding import PartitionSpec as P

precise = lax.Precision.HIGHEST


def phase_table(length, modes):
    points = lax.iota(jnp.int32, length)
    wrapped = points[:, None] * modes[None, :] % length
    angle = wrapped.astype(jnp.float32) * (2.0 * math.pi / length)
    return (jnp.cos(angle), jnp.sin(angle))


def gelu_slope(values):
    normal_cdf = 0.5 * (1.0 + lax.erf(values * 0.7071067811865476))
    density = jnp.exp(-0.5 * values * values) * 0.3989422804014327
    return normal_cdf + values * density


def channel_mix(blocks, spectrum):
    block_re = blocks[:, :, 0]
    block_im = blocks[:, :, 1]
    spec_re = spectrum[..., 0]
    spec_im = spectrum[..., 1]
    form = "baoc,czba->ozba"
    out_re = jnp.einsum(form, block_re, spec_re, precision=precise) - jnp.einsum(
        form, block_im, spec_im, precision=precise
    )
    out_im = jnp.einsum(form, block_re, spec_im, precision=precise) + jnp.einsum(
        form, block_im, spec_re, precision=precise
    )
    return jnp.stack([out_re, out_im], -1)


def channel_adjoint(blocks, spectrum):
    block_re = blocks[:, :, 0]
    block_im = blocks[:, :, 1]
    grad_re = spectrum[..., 0]
    grad_im = spectrum[..., 1]
    form = "baoc,ozba->czba"
    out_re = jnp.einsum(form, block_re, grad_re, precision=precise) + jnp.einsum(
        form, block_im, grad_im, precision=precise
    )
    out_im = jnp.einsum(form, block_re, grad_im, precision=precise) - jnp.einsum(
        form, block_im, grad_re, precision=precise
    )
    return jnp.stack([out_re, out_im], -1)


def block_gradient(spectrum_grad, spectrum):
    grad_re = spectrum_grad[..., 0]
    grad_im = spectrum_grad[..., 1]
    spec_re = spectrum[..., 0]
    spec_im = spectrum[..., 1]
    form = "ozba,czba->aboc"
    out_re = jnp.einsum(form, grad_re, spec_re, precision=precise) + jnp.einsum(
        form, grad_im, spec_im, precision=precise
    )
    out_im = jnp.einsum(form, grad_im, spec_re, precision=precise) - jnp.einsum(
        form, grad_re, spec_im, precision=precise
    )
    return jnp.stack([out_re, out_im], 2)


def invert_rows(spectrum, cos_rows, sin_rows):
    spec_re = spectrum[..., 0]
    spec_im = spectrum[..., 1]
    form = "czma,xa->czmx"
    back_re = jnp.einsum(form, spec_re, cos_rows, precision=precise) - jnp.einsum(
        form, spec_im, sin_rows, precision=precise
    )
    back_im = jnp.einsum(form, spec_re, sin_rows, precision=precise) + jnp.einsum(
        form, spec_im, cos_rows, precision=precise
    )
    joined = jnp.stack([back_re, back_im], 3)
    return joined.reshape(joined.shape[0], joined.shape[1], 2 * joined.shape[2], joined.shape[4])


def on_device(
    field_in,
    cotangent,
    spectrum_saved,
    weight_store,
    block_slot,
    kx_modes,
    ky_modes,
    pointwise,
    bias_vector,
):
    channels, planes, rows_x, width_y = field_in.shape
    full_x = rows_x * lax.axis_size("px")
    modes_y = ky_modes.shape[0]
    local_y = modes_y // lax.axis_size("px")
    capacity = weight_store.shape[0]
    factor = 1.0 / math.sqrt(full_x * width_y)
    cos_y, sin_y = phase_table(width_y, ky_modes)
    table_y = jnp.stack([cos_y, -sin_y], 2).reshape(width_y, 2 * modes_y)
    cos_x, sin_x = phase_table(full_x, kx_modes)
    store_row, slots_row = (
        lax.all_gather(weight_store, "py", axis=0, tiled=True),
        lax.all_gather(block_slot, "py", axis=0, tiled=True),
    )
    slots_flat = slots_row.reshape(-1)

    def inverse_planes(spectrum):
        joined = invert_rows(spectrum, cos_x, sin_x)
        returned = lax.all_to_all(joined, "px", split_axis=3, concat_axis=2, tiled=True)
        return factor * jnp.einsum("czkx,yk->czxy", returned, table_y, precision=precise)

    weight_full = pointwise.astype(jnp.float32)
    local_x = block_slot.shape[0]
    indices = jnp.transpose(block_slot).reshape(-1)
    blocks = jnp.take(store_row, indices, axis=0).reshape(local_y, local_x, 2, channels, channels)
    mixed = channel_mix(blocks, spectrum_saved)

    def from_modes(spectrum):
        return lax.all_to_all(spectrum, "py", split_axis=1, concat_axis=3, tiled=True)

    spectral = inverse_planes(from_modes(mixed))
    mapped = jnp.einsum("oc,czxy->ozxy", pointwise, field_in, preferred_element_type=jnp.float32)
    grad = cotangent.astype(jnp.float32) * gelu_slope(
        mapped + bias_vector.reshape(channels, 1, 1, 1) + spectral
    )
    partial_value = jnp.einsum("czxy,yk->czkx", grad, table_y, precision=precise)
    moved = lax.all_to_all(partial_value, "px", split_axis=2, concat_axis=3, tiled=True)
    pieces = moved.reshape(channels, planes, local_y, 2, full_x)
    part_re = pieces[:, :, :, 0]
    part_im = pieces[:, :, :, 1]
    form = "czmx,xk->czmk"
    real_part = jnp.einsum(form, part_re, cos_x, precision=precise) + jnp.einsum(
        form, part_im, sin_x, precision=precise
    )
    imag_part = jnp.einsum(form, part_im, cos_x, precision=precise) - jnp.einsum(
        form, part_re, sin_x, precision=precise
    )
    spectrum_grad = lax.all_to_all(
        factor * jnp.stack([real_part, imag_part], -1),
        "py",
        split_axis=3,
        concat_axis=1,
        tiled=True,
    )
    input_spectrum = channel_adjoint(blocks, spectrum_grad)
    local_grad = block_gradient(spectrum_grad, spectrum_saved)
    field_grad = jnp.einsum("oc,ozxy->czxy", weight_full, grad, precision=precise) + inverse_planes(
        from_modes(input_spectrum)
    )
    grads_all = lax.all_gather(local_grad, "py", axis=0, tiled=True)
    grads_flat = grads_all.reshape(slots_flat.shape[0], 2 * channels * channels)
    targets = lax.axis_index("py") * capacity + lax.iota(jnp.int32, capacity)
    select = (targets[:, None] == slots_flat[None, :]).astype(jnp.float32)
    store_flat = jnp.dot(select, grads_flat, precision=precise)
    store_grad = store_flat.reshape(capacity, 2, channels, channels)
    return (field_grad, store_grad)


def solution(mesh):
    placed = (
        P(None, "py", "px", None),
        P(None, "py", "px", None),
        P(None, None, "px", "py", None),
        P(("px", "py"), None, None, None),
        P("py", "px"),
        P(),
        P(),
        P(),
        P(),
    )
    return jax.shard_map(
        on_device,
        mesh=mesh,
        in_specs=placed,
        out_specs=(P(None, "py", "px", None), P(("px", "py"), None, None, None)),
        check_vma=False,
    )
```

profile of v0, /device:TPU:64, one launch (start us, length us, event | category | flops | bytes accessed | tf_op | source)
XLA Modules:
  0.0 343.6 jit_solution(8667537079059800114)
XLA Ops:
  10.2 91.8 %all-gather.3.cloned.1.call-done = f32[128,2,32,32]{3,2,1,0:T(8,128)} async-done(((f32[4,2,32,32]{3,2,1,0:T(8,128)}), f32[128,2,32,32]{3,2,1,0:T(8,128)}) %all-gather.3.cloned.1.call-update) | async-done | bytes 1048592 | tf_op jit(solution)/shard_map/all_gather | solution.py:103
  102.0 2.7 gather_fusion
  105.8 15.5 %all_to_all.99 = f32[32,1,128]{2,1,0:T(1,128)S(1)} all-to-all(f32[32,1,128]{2,1,0:T(1,128)S(1)} %reshape.429), channel_id=1, replica_groups=mesh['px'=16,'py'=32] {'py'}, dimensions={0} | all-to-all | bytes 32768 | tf_op jit(solution)/shard_map/all_to_all | solution.py:120
  128.2 7.8 %all-to-all-start.1 = ((f32[16,1,4096]{2,1,0:T(1,128)}), f32[16,1,4096]{2,1,0:T(1,128)S(1)}, u32[]{:S(2)}, u32[]{:S(2)}) async-start(f32[16,1,4096]{2,1,0:T(1,128)} %reshape.431), calls=%async_computation.1 | async-start | bytes 524288 | tf_op jit(solution)/shard_map/all_to_all | solution.py:110
  138.8 6.8 %all-to-all-done.1 = f32[16,1,4096]{2,1,0:T(1,128)S(1)} async-done(((f32[16,1,4096]{2,1,0:T(1,128)}), f32[16,1,4096]{2,1,0:T(1,128)S(1)}, u32[]{:S(2)}, u32[]{:S(2)}) %all-to-all-start.1) | async-done | bytes 262176 | tf_op jit(solution)/shard_map/all_to_all | solution.py:110
  149.2 6.6 %fusion.6 = f32[32,32,512]{2,0,1:T(8,128)S(1)} fusion(f32[32,32,512]{2,0,1:T(8,128)} %fusion.25, f32[32,64,32]{1,0,2:T(8,128)S(1)} %copy.172, f32[512,64,1]{0,1,2:T(8,128)S(1)} %reshape.416, bf16[32,1,32,512]{3,2,1,0:T(8,128)(2,1)} %param.10, f32[32]{0:T(128)S(1)} %copy-done.5), kind=kOutput, calls=%fused_computation.8 | convolution fusion | flops 409468928 | bytes 5636224 | tf_op jit(solution)/shard_map/czkx,yk->czxy/dot_general | solution.py:111
  157.1 2.6 fusion.10
  161.8 5.0 %all-to-all-start.2 = ((f32[16,1,4096]{2,1,0:T(1,128)}), f32[16,1,4096]{2,1,0:T(1,128)S(1)}, u32[]{:S(2)}, u32[]{:S(2)}) async-start(f32[16,1,4096]{2,1,0:T(1,128)} %reshape.433), calls=%async_computation.2 | async-start | bytes 524288 | tf_op jit(solution)/shard_map/all_to_all | solution.py:128
  166.8 33.0 %all-gather = s32[32,1,2]{2,1,0:T(1,128)S(1)} all-gather(s32[1,1,2]{2,1,0:T(1,128)S(1)} %bitcast.269), channel_id=1, replica_groups=mesh['px'=16,'py'=32] {'py'}, dimensions={0}, use_global_device_ids=true | all-gather | bytes 264 | tf_op jit(solution)/shard_map/all_gather | solution.py:104
  206.9 4.9 %all-to-all-start.3 = ((f32[32,1,128]{2,1,0:T(1,128)}), f32[32,1,128]{2,1,0:T(1,128)S(1)}, u32[]{:S(2)}, u32[]{:S(2)}) async-start(f32[32,1,128]{2,1,0:T(1,128)} %reshape.435), calls=%async_computation.3 | async-start | bytes 32768 | tf_op jit(solution)/shard_map/all_to_all | solution.py:139
  211.9 2.9 fusion.78
  214.8 6.8 %all-to-all-done.3 = f32[32,1,128]{2,1,0:T(1,128)S(1)} async-done(((f32[32,1,128]{2,1,0:T(1,128)}), f32[32,1,128]{2,1,0:T(1,128)S(1)}, u32[]{:S(2)}, u32[]{:S(2)}) %all-to-all-start.3) | async-done | bytes 16416 | tf_op jit(solution)/shard_map/all_to_all | solution.py:139
  224.7 3.8 %all-to-all-start.4 = ((f32[32,1,128]{2,1,0:T(1,128)}), f32[32,1,128]{2,1,0:T(1,128)S(1)}, u32[]{:S(2)}, u32[]{:S(2)}) async-start(f32[32,1,128]{2,1,0:T(1,128)} %reshape.437), calls=%async_computation.4 | async-start | bytes 32768 | tf_op jit(solution)/shard_map/all_to_all | solution.py:120
  228.8 9.5 %all-to-all-done.4 = f32[32,1,128]{2,1,0:T(1,128)S(1)} async-done(((f32[32,1,128]{2,1,0:T(1,128)}), f32[32,1,128]{2,1,0:T(1,128)S(1)}, u32[]{:S(2)}, u32[]{:S(2)}) %all-to-all-start.4) | async-done | bytes 16416 | tf_op jit(solution)/shard_map/all_to_all | solution.py:120
  244.4 2.6 reshape.439
  247.0 7.3 %all-to-all-start.5 = ((f32[16,1,4096]{2,1,0:T(1,128)}), f32[16,1,4096]{2,1,0:T(1,128)}, u32[]{:S(2)}, u32[]{:S(2)}) async-start(f32[16,1,4096]{2,1,0:T(1,128)} %reshape.439), calls=%async_computation.5 | async-start | bytes 524288 | tf_op jit(solution)/shard_map/all_to_all | solution.py:110
  254.3 54.2 %all_gather.11 = f32[32,2,2,32,32]{4,3,2,1,0:T(8,128)} all-gather(f32[1,2,2,32,32]{4,3,2,1,0:T(8,128)S(1)} %copy.168), channel_id=1, replica_groups=mesh['px'=16,'py'=32] {'py'}, dimensions={0}, use_global_device_ids=true | all-gather | bytes 540672 | tf_op jit(solution)/shard_map/all_gather | solution.py:151
  308.5 3.1 reshape.401
  314.0 3.4 fusion.81
  318.0 3.0 reduce.9
  323.4 2.6 copy.185
  328.6 2.7 copy.175
  331.2 2.9 fusion.7
  334.2 2.5 copy.170
  (99 shorter events, 44.9 us)
Async XLA Ops:
  7.2 129.4 %copy-start = (bf16[32,1,32,512]{3,2,1,0:T(8,128)(2,1)S(1)}, bf16[32,1,32,512]{3,2,1,0:T(8,128)(2,1)}, u32[]{:S(2)}) copy-start(bf16[32,1,32,512]{3,2,1,0:T(8,128)(2,1)} %param.9) | copy-start | bytes 3145732
  7.2 118.1 %copy-start.6 = (s32[32]{0:T(128)S(1)}, s32[32]{0:T(128)}, u32[]{:S(2)}) copy-start(s32[32]{0:T(128)} %param.14) | copy-start | bytes 388
  7.2 94.9 %all-gather.3.cloned.1.call-start = ((), (), s32[]{:S(2)}) async-start(), calls=%async_computation.6 | async-start | bytes 4325376 | tf_op jit(solution)/shard_map/all_gather | solution.py:103
  126.4 9.6 %copy-start.3 = (s32[32]{0:T(128)S(1)}, s32[32]{0:T(128)}, u32[]{:S(2)}) copy-start(s32[32]{0:T(128)} %param.15) | copy-start | bytes 388
  126.5 10.1 %copy-start.2 = (bf16[32,32]{1,0:T(8,128)(2,1)S(1)}, bf16[32,32]{1,0:T(8,128)(2,1)}, u32[]{:S(2)}) copy-start(bf16[32,32]{1,0:T(8,128)(2,1)} %param.16) | copy-start | bytes 6148
  128.2 17.4 %all-to-all-start.1 = ((f32[16,1,4096]{2,1,0:T(1,128)}), f32[16,1,4096]{2,1,0:T(1,128)S(1)}, u32[]{:S(2)}, u32[]{:S(2)}) async-start(f32[16,1,4096]{2,1,0:T(1,128)} %reshape.431), calls=%async_computation.1 | async-start | bytes 524288 | tf_op jit(solution)/shard_map/all_to_all | solution.py:110
  148.0 1.1 copy-start.5
  155.8 1.3 copy-start.1
  159.7 7.1 %copy-start.4 = (s32[1,2]{1,0:T(1,128)S(1)}, s32[1,2]{1,0:T(1,128)}, u32[]{:S(2)}) copy-start(s32[1,2]{1,0:T(1,128)} %param.13) | copy-start | bytes 28
  161.8 39.2 %all-to-all-start.2 = ((f32[16,1,4096]{2,1,0:T(1,128)}), f32[16,1,4096]{2,1,0:T(1,128)S(1)}, u32[]{:S(2)}, u32[]{:S(2)}) async-start(f32[16,1,4096]{2,1,0:T(1,128)} %reshape.433), calls=%async_computation.2 | async-start | bytes 524288 | tf_op jit(solution)/shard_map/all_to_all | solution.py:128
  206.9 14.7 %all-to-all-start.3 = ((f32[32,1,128]{2,1,0:T(1,128)}), f32[32,1,128]{2,1,0:T(1,128)S(1)}, u32[]{:S(2)}, u32[]{:S(2)}) async-start(f32[32,1,128]{2,1,0:T(1,128)} %reshape.435), calls=%async_computation.3 | async-start | bytes 32768 | tf_op jit(solution)/shard_map/all_to_all | solution.py:139
  224.7 13.6 %all-to-all-start.4 = ((f32[32,1,128]{2,1,0:T(1,128)}), f32[32,1,128]{2,1,0:T(1,128)S(1)}, u32[]{:S(2)}, u32[]{:S(2)}) async-start(f32[32,1,128]{2,1,0:T(1,128)} %reshape.437), calls=%async_computation.4 | async-start | bytes 32768 | tf_op jit(solution)/shard_map/all_to_all | solution.py:120
  247.0 71.0 %all-to-all-start.5 = ((f32[16,1,4096]{2,1,0:T(1,128)}), f32[16,1,4096]{2,1,0:T(1,128)}, u32[]{:S(2)}, u32[]{:S(2)}) async-start(f32[16,1,4096]{2,1,0:T(1,128)} %reshape.439), calls=%async_computation.5 | async-start | bytes 524288 | tf_op jit(solution)/shard_map/all_to_all | solution.py:110
Sparse Core Ops, SparseCore 0:
  11.2 90.8 all-gather.2
where the time goes:
time: 345 us; the launch traced here: 344 us
  waiting for transfers between devices  116 us (34%)
  blocking collectives  103 us (30%)
  local copies, waits for them, and re-layouts  40.7 us (12%)
  matrix products  30.9 us (9%)
  starting transfers between devices  28.8 us (8%)
  between operations  14.6 us (4%)
  other arithmetic  10.3 us (3%)
    all_gather x1, waiting for transfers between devices, on_device(): lax.all_gather(weight_store, 'py', axis=0, tiled=True)  91.8 us
    all_gather x1, blocking collectives, on_device(): grads_all = lax.all_gather(local_grad, 'py', axis=0, tiled=True)  54.2 us
    all_gather x1, blocking collectives, on_device(): lax.all_gather(block_slot, 'py', axis=0, tiled=True)  33 us
    all_to_all x1, blocking collectives, from_modes(): lax.all_to_all(spectrum, 'py', split_axis=1, concat_axis=3, tiled=True)  15.5 us
    all_to_all x2, starting transfers between devices, inverse_planes(): lax.all_to_all(joined, 'px', split_axis=3, concat_axis=2, tiled=True)  15 us
    unnamed x28, local copies, waits for them, and re-layouts  14.9 us
    dot_general x2, matrix products, inverse_planes(): jnp.einsum('czkx,yk->czxy', returned, table_y, precision=precise)  9.54 us
    all_to_all x1, waiting for transfers between devices, from_modes(): lax.all_to_all(spectrum, 'py', split_axis=1, concat_axis=3, tiled=True)  9.47 us
  transfers between devices with their start and end apart: 6, of which 4 were waited for; matrix products, arithmetic and copies ran while one was open for 6% of the time, Pallas kernels for 0%

commit v1 on v0

--- a/solution.py
+++ b/solution.py
@@ -101,7 +101,9 @@
     cos_x, sin_x = phase_table(full_x, kx_modes)
     store_row, slots_row = (
         lax.all_gather(weight_store, "py", axis=0, tiled=True),
-        lax.all_gather(block_slot, "py", axis=0, tiled=True),
+        jnp.concatenate(
+            lax.all_to_all(jnp.stack([block_slot] * lax.axis_size("py")), "py", 0, 0), axis=0
+        ),
     )
     slots_flat = slots_row.reshape(-1)
 

time: 345 us -> 327 us (0.948)
  the two profiles are of different devices: /device:TPU:64 before, /device:TPU:2 now
where the time goes in v1:
time: 327 us; the launch traced here: 326 us
  waiting for transfers between devices  124 us (38%)
  blocking collectives  70.4 us (22%)
  local copies, waits for them, and re-layouts  41.2 us (13%)
  starting transfers between devices  35.2 us (11%)
  matrix products  30.9 us (9%)
  between operations  14.7 us (4%)
  other arithmetic  9.43 us (3%)
    all_gather x1, waiting for transfers between devices, on_device(): lax.all_gather(weight_store, 'py', axis=0, tiled=True)  91.3 us
    all_gather x1, blocking collectives, on_device(): grads_all = lax.all_gather(local_grad, 'py', axis=0, tiled=True)  54.5 us
    all_to_all x1, blocking collectives, from_modes(): lax.all_to_all(spectrum, 'py', split_axis=1, concat_axis=3, tiled=True)  15.9 us
    unnamed x28, local copies, waits for them, and re-layouts  14.9 us
    all_to_all x2, starting transfers between devices, inverse_planes(): lax.all_to_all(joined, 'px', split_axis=3, concat_axis=2, tiled=True)  11.7 us
    all_to_all x1, starting transfers between devices, on_device(): lax.all_to_all(factor * jnp.stack([real_part, imag_part], -1), 'py', spli...  9.85 us
    all_to_all x1, waiting for transfers between devices, on_device(): lax.all_to_all(partial_value, 'px', split_axis=2, concat_axis=3, tiled=True)  9.63 us
    dot_general x2, matrix products, inverse_planes(): jnp.einsum('czkx,yk->czxy', returned, table_y, precision=precise)  9.54 us
  transfers between devices with their start and end apart: 7, of which 5 were waited for; matrix products, arithmetic and copies ran while one was open for 10% of the time, Pallas kernels for 0%

profile of v1, /device:TPU:2, one launch (start us, length us, event | category | flops | bytes accessed | tf_op | source)
XLA Modules:
  0.0 325.8 jit_solution(312264391533539523)
XLA Ops:
  10.2 91.3 %all-gather.2.cloned.1.call-done = f32[128,2,32,32]{3,2,1,0:T(8,128)} async-done(((f32[4,2,32,32]{3,2,1,0:T(8,128)}), f32[128,2,32,32]{3,2,1,0:T(8,128)}) %all-gather.2.cloned.1.call-update) | async-done | bytes 1048592 | tf_op jit(solution)/shard_map/all_gather | solution.py:103
  101.5 2.7 gather_fusion
  105.3 15.9 %all_to_all.104 = f32[32,1,128]{2,1,0:T(1,128)S(1)} all-to-all(f32[32,1,128]{2,1,0:T(1,128)S(1)} %reshape.429), channel_id=1, replica_groups=mesh['px'=16,'py'=32] {'py'}, dimensions={0} | all-to-all | bytes 32768 | tf_op jit(solution)/shard_map/all_to_all | solution.py:122
  127.8 7.5 %all-to-all-start.1 = ((f32[16,1,4096]{2,1,0:T(1,128)}), f32[16,1,4096]{2,1,0:T(1,128)S(1)}, u32[]{:S(2)}, u32[]{:S(2)}) async-start(f32[16,1,4096]{2,1,0:T(1,128)} %reshape.431), calls=%async_computation.1 | async-start | bytes 524288 | tf_op jit(solution)/shard_map/all_to_all | solution.py:112
  138.1 8.3 %all-to-all-done.1 = f32[16,1,4096]{2,1,0:T(1,128)S(1)} async-done(((f32[16,1,4096]{2,1,0:T(1,128)}), f32[16,1,4096]{2,1,0:T(1,128)S(1)}, u32[]{:S(2)}, u32[]{:S(2)}) %all-to-all-start.1) | async-done | bytes 262176 | tf_op jit(solution)/shard_map/all_to_all | solution.py:112
  147.1 4.9 %all-to-all-start.6 = ((s32[32,1,2]{2,1,0:T(1,128)}), s32[32,1,2]{2,1,0:T(1,128)S(1)}, u32[]{:S(2)}, u32[]{:S(2)}) async-start(s32[32,1,2]{2,1,0:T(1,128)} %stack.110), calls=%async_computation.6 | async-start | bytes 32768 | tf_op jit(solution)/shard_map/all_to_all | solution.py:105
  155.4 6.6 %fusion.6 = f32[32,32,512]{2,0,1:T(8,128)S(1)} fusion(f32[32,32,512]{2,0,1:T(8,128)} %fusion.25, f32[32,64,32]{1,0,2:T(8,128)S(1)} %copy.172, f32[512,64,1]{0,1,2:T(8,128)S(1)} %reshape.416, bf16[32,1,32,512]{3,2,1,0:T(8,128)(2,1)} %param.10, f32[32]{0:T(128)S(1)} %copy-done.5), kind=kOutput, calls=%fused_computation.8 | convolution fusion | flops 409468928 | bytes 5636224 | tf_op jit(solution)/shard_map/czkx,yk->czxy/dot_general | solution.py:113
  163.4 2.6 fusion.10
  168.1 3.8 %all-to-all-start.2 = ((f32[16,1,4096]{2,1,0:T(1,128)}), f32[16,1,4096]{2,1,0:T(1,128)S(1)}, u32[]{:S(2)}, u32[]{:S(2)}) async-start(f32[16,1,4096]{2,1,0:T(1,128)} %reshape.433), calls=%async_computation.2 | async-start | bytes 524288 | tf_op jit(solution)/shard_map/all_to_all | solution.py:130
  173.2 9.6 %all-to-all-done.2 = f32[16,1,4096]{2,1,0:T(1,128)S(1)} async-done(((f32[16,1,4096]{2,1,0:T(1,128)}), f32[16,1,4096]{2,1,0:T(1,128)S(1)}, u32[]{:S(2)}, u32[]{:S(2)}) %all-to-all-start.2) | async-done | bytes 262176 | tf_op jit(solution)/shard_map/all_to_all | solution.py:130
  188.5 9.9 %all-to-all-start.3 = ((f32[32,1,128]{2,1,0:T(1,128)}), f32[32,1,128]{2,1,0:T(1,128)S(1)}, u32[]{:S(2)}, u32[]{:S(2)}) async-start(f32[32,1,128]{2,1,0:T(1,128)} %reshape.435), calls=%async_computation.3 | async-start | bytes 32768 | tf_op jit(solution)/shard_map/all_to_all | solution.py:141
  198.4 2.9 fusion.78
  201.3 5.7 %all-to-all-done.3 = f32[32,1,128]{2,1,0:T(1,128)S(1)} async-done(((f32[32,1,128]{2,1,0:T(1,128)}), f32[32,1,128]{2,1,0:T(1,128)S(1)}, u32[]{:S(2)}, u32[]{:S(2)}) %all-to-all-start.3) | async-done | bytes 16416 | tf_op jit(solution)/shard_map/all_to_all | solution.py:141
  209.9 4.9 %all-to-all-start.4 = ((f32[32,1,128]{2,1,0:T(1,128)}), f32[32,1,128]{2,1,0:T(1,128)S(1)}, u32[]{:S(2)}, u32[]{:S(2)}) async-start(f32[32,1,128]{2,1,0:T(1,128)} %reshape.437), calls=%async_computation.4 | async-start | bytes 32768 | tf_op jit(solution)/shard_map/all_to_all | solution.py:122
  215.0 8.4 %all-to-all-done.4 = f32[32,1,128]{2,1,0:T(1,128)S(1)} async-done(((f32[32,1,128]{2,1,0:T(1,128)}), f32[32,1,128]{2,1,0:T(1,128)S(1)}, u32[]{:S(2)}, u32[]{:S(2)}) %all-to-all-start.4) | async-done | bytes 16416 | tf_op jit(solution)/shard_map/all_to_all | solution.py:122
  229.4 2.6 reshape.439
  232.0 4.2 %all-to-all-start.5 = ((f32[16,1,4096]{2,1,0:T(1,128)}), f32[16,1,4096]{2,1,0:T(1,128)}, u32[]{:S(2)}, u32[]{:S(2)}) async-start(f32[16,1,4096]{2,1,0:T(1,128)} %reshape.439), calls=%async_computation.5 | async-start | bytes 524288 | tf_op jit(solution)/shard_map/all_to_all | solution.py:112
  236.3 54.5 %all_gather.7 = f32[32,2,2,32,32]{4,3,2,1,0:T(8,128)} all-gather(f32[1,2,2,32,32]{4,3,2,1,0:T(8,128)S(1)} %copy.168), channel_id=1, replica_groups=mesh['px'=16,'py'=32] {'py'}, dimensions={0}, use_global_device_ids=true | all-gather | bytes 540672 | tf_op jit(solution)/shard_map/all_gather | solution.py:153
  290.8 3.1 reshape.404
  296.3 3.4 %fusion.81 = f32[4,2,32,32]{3,0,2,1:T(4,128)S(1)} fusion(f32[2,32,32,64]{3,2,1,0:T(8,128)} %bitcast.238, s32[64]{0:T(128)S(1)} %eq.19, s32[4]{0:T(128)S(1)} %iota_add_fusion), kind=kOutput, calls=%fused_computation.113 | convolution fusion | flops 6291712 | bytes 557328 | tf_op jit(solution)/shard_map/dot_general | solution.py:157
  300.3 2.8 reduce.9
  305.6 2.6 copy.185
  310.7 2.7 copy.175
  313.4 2.9 fusion.7
  (101 shorter events, 47.3 us)
Async XLA Ops:
  7.2 128.7 %copy-start = (bf16[32,1,32,512]{3,2,1,0:T(8,128)(2,1)S(1)}, bf16[32,1,32,512]{3,2,1,0:T(8,128)(2,1)}, u32[]{:S(2)}) copy-start(bf16[32,1,32,512]{3,2,1,0:T(8,128)(2,1)} %param.9) | copy-start | bytes 3145732
  7.2 117.7 %copy-start.6 = (s32[32]{0:T(128)S(1)}, s32[32]{0:T(128)}, u32[]{:S(2)}) copy-start(s32[32]{0:T(128)} %param.14) | copy-start | bytes 388
  7.2 94.3 %all-gather.2.cloned.1.call-start = ((), (), s32[]{:S(2)}) async-start(), calls=%async_computation.7 | async-start | bytes 4325376 | tf_op jit(solution)/shard_map/all_gather | solution.py:103
  126.0 9.3 %copy-start.3 = (s32[32]{0:T(128)S(1)}, s32[32]{0:T(128)}, u32[]{:S(2)}) copy-start(s32[32]{0:T(128)} %param.15) | copy-start | bytes 388
  126.1 9.9 %copy-start.2 = (bf16[32,32]{1,0:T(8,128)(2,1)S(1)}, bf16[32,32]{1,0:T(8,128)(2,1)}, u32[]{:S(2)}) copy-start(bf16[32,32]{1,0:T(8,128)(2,1)} %param.16) | copy-start | bytes 6148
  127.8 18.7 %all-to-all-start.1 = ((f32[16,1,4096]{2,1,0:T(1,128)}), f32[16,1,4096]{2,1,0:T(1,128)S(1)}, u32[]{:S(2)}, u32[]{:S(2)}) async-start(f32[16,1,4096]{2,1,0:T(1,128)} %reshape.431), calls=%async_computation.1 | async-start | bytes 524288 | tf_op jit(solution)/shard_map/all_to_all | solution.py:112
  135.3 11.2 %copy-start.4 = (s32[1,2]{1,0:T(1,128)S(1)}, s32[1,2]{1,0:T(1,128)}, u32[]{:S(2)}) copy-start(s32[1,2]{1,0:T(1,128)} %param.13) | copy-start | bytes 28
  147.1 21.0 %all-to-all-start.6 = ((s32[32,1,2]{2,1,0:T(1,128)}), s32[32,1,2]{2,1,0:T(1,128)S(1)}, u32[]{:S(2)}, u32[]{:S(2)}) async-start(s32[32,1,2]{2,1,0:T(1,128)} %stack.110), calls=%async_computation.6 | async-start | bytes 32768 | tf_op jit(solution)/shard_map/all_to_all | solution.py:105
  154.3 1.1 copy-start.5
  162.0 1.3 copy-start.1
  168.1 14.7 %all-to-all-start.2 = ((f32[16,1,4096]{2,1,0:T(1,128)}), f32[16,1,4096]{2,1,0:T(1,128)S(1)}, u32[]{:S(2)}, u32[]{:S(2)}) async-start(f32[16,1,4096]{2,1,0:T(1,128)} %reshape.433), calls=%async_computation.2 | async-start | bytes 524288 | tf_op jit(solution)/shard_map/all_to_all | solution.py:130
  188.5 18.4 %all-to-all-start.3 = ((f32[32,1,128]{2,1,0:T(1,128)}), f32[32,1,128]{2,1,0:T(1,128)S(1)}, u32[]{:S(2)}, u32[]{:S(2)}) async-start(f32[32,1,128]{2,1,0:T(1,128)} %reshape.435), calls=%async_computation.3 | async-start | bytes 32768 | tf_op jit(solution)/shard_map/all_to_all | solution.py:141
  209.9 13.5 %all-to-all-start.4 = ((f32[32,1,128]{2,1,0:T(1,128)}), f32[32,1,128]{2,1,0:T(1,128)S(1)}, u32[]{:S(2)}, u32[]{:S(2)}) async-start(f32[32,1,128]{2,1,0:T(1,128)} %reshape.437), calls=%async_computation.4 | async-start | bytes 32768 | tf_op jit(solution)/shard_map/all_to_all | solution.py:122
  232.0 68.3 %all-to-all-start.5 = ((f32[16,1,4096]{2,1,0:T(1,128)}), f32[16,1,4096]{2,1,0:T(1,128)}, u32[]{:S(2)}, u32[]{:S(2)}) async-start(f32[16,1,4096]{2,1,0:T(1,128)} %reshape.439), calls=%async_computation.5 | async-start | bytes 524288 | tf_op jit(solution)/shard_map/all_to_all | solution.py:112
Sparse Core Ops, SparseCore 0:
  11.2 90.2 all-gather.1
